TPU v7x, 32 devices: a whole 2x2x4 slice. The times are simulated.
32 devices in a mesh: pair: 8 (over y, x, core), ints: 4 (over z).
Axes of the slice: x: 2, y: 2, z: 4, core: 2. Of those that a mesh axis runs over, the one named last changes fastest.
Arguments:
- t_amps: bfloat16 [32, 8, 4096], P('pair', None, 'ints'), may hold values from -6 to 6
- block_mask: int32 [32, 8, 64], P('pair', None, 'ints'), may hold values 0 or 1
- factors: bfloat16 [8, 64, 64, 128], P('pair', 'ints'), may hold values from -0.75 to 0.75
- links: int32 [8, 64, 32], P('pair', 'ints'), may hold values from 0 to 63, as said below
- link_counts: int32 [8, 64], P('pair', 'ints'), may hold values from 8 to 32, as said below
Outputs:
- ladder: bfloat16 [32, 8, 4096], P('pair', None, 'ints')
Inputs may be any that keep to these rules, and one draw needn't show every extreme that they name: `links`: the 32 slots of a tile name distinct tiles of its own block; only the first link_counts slots are used. `link_counts`: in every block, tile 0 uses all 32 slots.
All inputs are finite; a program needn't handle non-finite values. No bound on the sum of `block_mask` on one device may be relied on, other than what follows from the above.
Results may differ from a plain program's by a relative error of at most 0.008.
Values may be sent and summed in bfloat16 or wider, within the bound.
A program may use at most 128 MiB of HBM per device.

v0:
```python
import jax
import jax.numpy as jnp
from jax import lax
from jax.sharding import PartitionSpec as P


def split_high(values):
    high = values.astype(jnp.bfloat16)
    rest = (values - high.astype(jnp.float32)).astype(jnp.bfloat16)
    return (high, rest)


def tile_ladder(all_f, all_t, own_f, link_rows, count_rows):
    slots = jnp.arange(link_rows.shape[-1], dtype=jnp.int32)
    npairs = all_t.shape[0]
    tile = own_f.shape[1]
    amp_tiles = all_t.reshape(npairs, all_f.shape[0], tile)

    def one_tile(inputs):
        own, index_row, count = inputs
        near_f = jnp.take(all_f, index_row, axis=0)
        near_t = jnp.take(amp_tiles, index_row, axis=1)
        used = (slots < count).astype(jnp.float32)
        blocks = jnp.einsum("xq,kyq->kxy", own, near_f, preferred_element_type=jnp.float32)
        blocks = blocks * used[:, None, None]
        high, rest = split_high(blocks)
        first = jnp.einsum("kxy,pky->px", high, near_t, preferred_element_type=jnp.float32)
        second = jnp.einsum("kxy,pky->px", rest, near_t, preferred_element_type=jnp.float32)
        return first + second

    stacked = lax.map(one_tile, (own_f, link_rows, count_rows))
    return jnp.transpose(stacked, (1, 0, 2)).reshape(npairs, own_f.shape[0] * tile)


def body(t_amps, block_mask, factors, links, link_counts):
    own_f = factors[0]
    link_rows = links[0]
    count_rows = link_counts[0]
    tile_count = own_f.shape[0]
    tile = own_f.shape[1]
    pair_dev, nblocks, width = t_amps.shape
    shaped = t_amps.reshape(pair_dev, nblocks, tile_count, tile)
    masked = (shaped * block_mask[:, :, :, None].astype(t_amps.dtype)).reshape(
        pair_dev, nblocks, width
    )
    local = lax.all_to_all(masked, "pair", split_axis=1, concat_axis=0, tiled=True)[:, 0, :]
    all_f, all_t = (
        lax.all_gather(own_f, "ints", axis=0, tiled=True),
        lax.all_gather(local, "ints", axis=1, tiled=True),
    )
    result = tile_ladder(all_f, all_t, own_f, link_rows, count_rows)
    rounded = result.astype(jnp.bfloat16)[:, None, :]
    return lax.all_to_all(rounded, "pair", split_axis=0, concat_axis=1, tiled=True)


def solution(mesh):
    placed = (
        P("pair", None, "ints"),
        P("pair", None, "ints"),
        P("pair", "ints", None, None),
        P("pair", "ints", None),
        P("pair", "ints"),
    )
    return jax.shard_map(
        body, mesh=mesh, in_specs=placed, out_specs=P("pair", None, "ints"), check_vma=False
    )
```

profile of v0, /device:TPU:0, one launch (start us, length us, event | category | flops | bytes accessed | tf_op | source)
XLA Modules:
  0.0 173.7 jit_solution(7210912905600619136)
XLA Ops:
  6.5 0.7 all-gather.3.cloned.1.call-update
  9.0 5.2 %all-to-all-start = ((bf16[4,8,1024]{2,0,1:T(4,128)(2,1)}), bf16[4,8,1024]{2,0,1:T(4,128)(2,1)S(1)}, u32[]{:S(2)}, u32[]{:S(2)}) async-start(bf16[4,8,1024]{2,0,1:T(4,128)(2,1)} %copy.27), calls=%async_computation | async-start | bytes 131072 | tf_op jit(solution)/shard_map/all_to_all | solution.py:46
  14.2 5.0 %all-to-all-done = bf16[4,8,1024]{2,0,1:T(4,128)(2,1)S(1)} async-done(((bf16[4,8,1024]{2,0,1:T(4,128)(2,1)}), bf16[4,8,1024]{2,0,1:T(4,128)(2,1)S(1)}, u32[]{:S(2)}, u32[]{:S(2)}) %all-to-all-start) | async-done | bytes 65568 | tf_op jit(solution)/shard_map/all_to_all | solution.py:46
  19.2 16.7 %all_gather.6 = bf16[32,4096]{1,0:T(8,128)(2,1)S(1)} all-gather(bf16[32,1024]{1,0:T(8,128)(2,1)S(1)} %squeeze.27), channel_id=1, replica_groups=mesh['pair'=8,'ints'=4] {'ints'}, dimensions={1}, use_global_device_ids=true | all-gather | bytes 327680 | tf_op jit(solution)/shard_map/all_gather | solution.py:49
  36.8 7.0 %all-gather.3.cloned.1.call-done = bf16[1,64,64,128]{3,2,0,1:T(8,128)(2,1)} async-done(((bf16[1,16,64,128]{3,2,0,1:T(8,128)(2,1)}), bf16[1,64,64,128]{3,2,0,1:T(8,128)(2,1)}) %all-gather.3.cloned.1.call-update) | async-done | bytes 1048592 | tf_op jit(solution)/shard_map/all_gather | solution.py:48
  44.5 110.9 %while.11 = (s32[]{:T(128)}, bf16[16,32,64]{2,1,0:T(8,128)(2,1)S(1)}, s32[16,32]{1,0:T(8,128)}, bf16[32,64,64]{2,0,1:T(8,128)(2,1)S(1)}, bf16[64,64,128]{2,1,0:T...) while((s32[]{:T(128)}, bf16[16,32,64]{2,1,0:T(8,128)(2,1)S(1)}, ...), condition=%wide.region_1.2_spmd.clone, body=%wide.region_0.1_spmd.clone.sunk | while | flops 51514720 | bytes 4389073 | solution.py:31
  45.1 1.3 compare_convert_fusion.2
  46.4 0.7 fusion.33
  47.1 1.9 %gather_fusion = bf16[32,64,128]{2,1,0:T(8,128)(2,1)S(1)} fusion(bf16[64,64,128]{2,1,0:T(8,128)(2,1)} %get-tuple-element.168, s32[1024]{0:T(1024)S(1)} %pad_clamp_fusion.2), kind=kCustom, calls=%fused_computation.1.clone.clone.1 | custom fusion | bytes 1048704 | tf_op jit(solution)/shard_map/while/body/eval_jaxpr/jit(_take)/gather | solution.py:21
  49.0 1.1 fusion.34
  52.0 1.3 compare_convert_fusion.2
  53.4 0.7 fusion.33
  54.1 1.9 %gather_fusion = bf16[32,64,128]{2,1,0:T(8,128)(2,1)S(1)} fusion(bf16[64,64,128]{2,1,0:T(8,128)(2,1)} %get-tuple-element.168, s32[1024]{0:T(1024)S(1)} %pad_clamp_fusion.2), kind=kCustom, calls=%fused_computation.1.clone.clone.1 | custom fusion | bytes 1048704 | tf_op jit(solution)/shard_map/while/body/eval_jaxpr/jit(_take)/gather | solution.py:21
  55.9 1.1 fusion.34
  59.0 1.3 compare_convert_fusion.2
  60.3 0.7 fusion.33
  61.0 1.9 %gather_fusion = bf16[32,64,128]{2,1,0:T(8,128)(2,1)S(1)} fusion(bf16[64,64,128]{2,1,0:T(8,128)(2,1)} %get-tuple-element.168, s32[1024]{0:T(1024)S(1)} %pad_clamp_fusion.2), kind=kCustom, calls=%fused_computation.1.clone.clone.1 | custom fusion | bytes 1048704 | tf_op jit(solution)/shard_map/while/body/eval_jaxpr/jit(_take)/gather | solution.py:21
  62.9 1.1 fusion.34
  65.9 1.3 compare_convert_fusion.2
  67.9 1.9 %gather_fusion = bf16[32,64,128]{2,1,0:T(8,128)(2,1)S(1)} fusion(bf16[64,64,128]{2,1,0:T(8,128)(2,1)} %get-tuple-element.168, s32[1024]{0:T(1024)S(1)} %pad_clamp_fusion.2), kind=kCustom, calls=%fused_computation.1.clone.clone.1 | custom fusion | bytes 1048704 | tf_op jit(solution)/shard_map/while/body/eval_jaxpr/jit(_take)/gather | solution.py:21
  69.8 1.1 fusion.34
  72.8 1.3 compare_convert_fusion.2
  74.2 0.7 fusion.33
  74.9 1.9 %gather_fusion = bf16[32,64,128]{2,1,0:T(8,128)(2,1)S(1)} fusion(bf16[64,64,128]{2,1,0:T(8,128)(2,1)} %get-tuple-element.168, s32[1024]{0:T(1024)S(1)} %pad_clamp_fusion.2), kind=kCustom, calls=%fused_computation.1.clone.clone.1 | custom fusion | bytes 1048704 | tf_op jit(solution)/shard_map/while/body/eval_jaxpr/jit(_take)/gather | solution.py:21
  76.7 1.1 fusion.34
  79.7 1.3 compare_convert_fusion.2
  81.1 0.7 fusion.33
  81.8 1.9 %gather_fusion = bf16[32,64,128]{2,1,0:T(8,128)(2,1)S(1)} fusion(bf16[64,64,128]{2,1,0:T(8,128)(2,1)} %get-tuple-element.168, s32[1024]{0:T(1024)S(1)} %pad_clamp_fusion.2), kind=kCustom, calls=%fused_computation.1.clone.clone.1 | custom fusion | bytes 1048704 | tf_op jit(solution)/shard_map/while/body/eval_jaxpr/jit(_take)/gather | solution.py:21
  83.7 1.1 fusion.34
  86.7 1.3 compare_convert_fusion.2
  88.7 1.9 %gather_fusion = bf16[32,64,128]{2,1,0:T(8,128)(2,1)S(1)} fusion(bf16[64,64,128]{2,1,0:T(8,128)(2,1)} %get-tuple-element.168, s32[1024]{0:T(1024)S(1)} %pad_clamp_fusion.2), kind=kCustom, calls=%fused_computation.1.clone.clone.1 | custom fusion | bytes 1048704 | tf_op jit(solution)/shard_map/while/body/eval_jaxpr/jit(_take)/gather | solution.py:21
  90.6 1.1 fusion.34
  93.6 1.3 compare_convert_fusion.2
  95.0 0.7 fusion.33
  95.7 1.9 %gather_fusion = bf16[32,64,128]{2,1,0:T(8,128)(2,1)S(1)} fusion(bf16[64,64,128]{2,1,0:T(8,128)(2,1)} %get-tuple-element.168, s32[1024]{0:T(1024)S(1)} %pad_clamp_fusion.2), kind=kCustom, calls=%fused_computation.1.clone.clone.1 | custom fusion | bytes 1048704 | tf_op jit(solution)/shard_map/while/body/eval_jaxpr/jit(_take)/gather | solution.py:21
  97.5 1.1 fusion.34
  100.5 1.3 compare_convert_fusion.2
  101.9 0.7 fusion.33
  102.6 1.9 %gather_fusion = bf16[32,64,128]{2,1,0:T(8,128)(2,1)S(1)} fusion(bf16[64,64,128]{2,1,0:T(8,128)(2,1)} %get-tuple-element.168, s32[1024]{0:T(1024)S(1)} %pad_clamp_fusion.2), kind=kCustom, calls=%fused_computation.1.clone.clone.1 | custom fusion | bytes 1048704 | tf_op jit(solution)/shard_map/while/body/eval_jaxpr/jit(_take)/gather | solution.py:21
  104.5 1.1 fusion.34
  107.5 1.3 compare_convert_fusion.2
  108.8 0.7 fusion.33
  109.5 1.9 %gather_fusion = bf16[32,64,128]{2,1,0:T(8,128)(2,1)S(1)} fusion(bf16[64,64,128]{2,1,0:T(8,128)(2,1)} %get-tuple-element.168, s32[1024]{0:T(1024)S(1)} %pad_clamp_fusion.2), kind=kCustom, calls=%fused_computation.1.clone.clone.1 | custom fusion | bytes 1048704 | tf_op jit(solution)/shard_map/while/body/eval_jaxpr/jit(_take)/gather | solution.py:21
  111.4 1.1 fusion.34
  114.4 1.3 compare_convert_fusion.2
  116.4 1.9 %gather_fusion = bf16[32,64,128]{2,1,0:T(8,128)(2,1)S(1)} fusion(bf16[64,64,128]{2,1,0:T(8,128)(2,1)} %get-tuple-element.168, s32[1024]{0:T(1024)S(1)} %pad_clamp_fusion.2), kind=kCustom, calls=%fused_computation.1.clone.clone.1 | custom fusion | bytes 1048704 | tf_op jit(solution)/shard_map/while/body/eval_jaxpr/jit(_take)/gather | solution.py:21
  118.3 1.1 fusion.34
  121.3 1.3 compare_convert_fusion.2
  123.4 1.9 %gather_fusion = bf16[32,64,128]{2,1,0:T(8,128)(2,1)S(1)} fusion(bf16[64,64,128]{2,1,0:T(8,128)(2,1)} %get-tuple-element.168, s32[1024]{0:T(1024)S(1)} %pad_clamp_fusion.2), kind=kCustom, calls=%fused_computation.1.clone.clone.1 | custom fusion | bytes 1048704 | tf_op jit(solution)/shard_map/while/body/eval_jaxpr/jit(_take)/gather | solution.py:21
  125.3 1.1 fusion.34
  128.3 1.3 compare_convert_fusion.2
  130.3 1.9 %gather_fusion = bf16[32,64,128]{2,1,0:T(8,128)(2,1)S(1)} fusion(bf16[64,64,128]{2,1,0:T(8,128)(2,1)} %get-tuple-element.168, s32[1024]{0:T(1024)S(1)} %pad_clamp_fusion.2), kind=kCustom, calls=%fused_computation.1.clone.clone.1 | custom fusion | bytes 1048704 | tf_op jit(solution)/shard_map/while/body/eval_jaxpr/jit(_take)/gather | solution.py:21
  132.2 1.1 fusion.34
  135.2 1.3 compare_convert_fusion.2
  137.2 1.9 %gather_fusion = bf16[32,64,128]{2,1,0:T(8,128)(2,1)S(1)} fusion(bf16[64,64,128]{2,1,0:T(8,128)(2,1)} %get-tuple-element.168, s32[1024]{0:T(1024)S(1)} %pad_clamp_fusion.2), kind=kCustom, calls=%fused_computation.1.clone.clone.1 | custom fusion | bytes 1048704 | tf_op jit(solution)/shard_map/while/body/eval_jaxpr/jit(_take)/gather | solution.py:21
  139.1 1.1 fusion.34
  142.1 1.3 compare_convert_fusion.2
  144.2 1.9 %gather_fusion = bf16[32,64,128]{2,1,0:T(8,128)(2,1)S(1)} fusion(bf16[64,64,128]{2,1,0:T(8,128)(2,1)} %get-tuple-element.168, s32[1024]{0:T(1024)S(1)} %pad_clamp_fusion.2), kind=kCustom, calls=%fused_computation.1.clone.clone.1 | custom fusion | bytes 1048704 | tf_op jit(solution)/shard_map/while/body/eval_jaxpr/jit(_take)/gather | solution.py:21
  146.0 1.1 fusion.34
  149.1 1.3 compare_convert_fusion.2
  151.1 1.9 %gather_fusion = bf16[32,64,128]{2,1,0:T(8,128)(2,1)S(1)} fusion(bf16[64,64,128]{2,1,0:T(8,128)(2,1)} %get-tuple-element.168, s32[1024]{0:T(1024)S(1)} %pad_clamp_fusion.2), kind=kCustom, calls=%fused_computation.1.clone.clone.1 | custom fusion | bytes 1048704 | tf_op jit(solution)/shard_map/while/body/eval_jaxpr/jit(_take)/gather | solution.py:21
  153.0 1.1 fusion.34
  156.1 1.0 reduce.1
  157.1 8.6 %all_to_all.33 = bf16[8,2,2048]{2,1,0:T(2,128)(2,1)S(1)} all-to-all(bf16[8,2,2048]{2,1,0:T(2,128)(2,1)S(1)} %reshape.86), channel_id=1, replica_groups=mesh['pair'=8,'ints'=4] {'pair'}, dimensions={0} | all-to-all | bytes 131072 | tf_op jit(solution)/shard_map/all_to_all | solution.py:53
  (112 shorter events, 41.1 us)
Async XLA Ops:
  6.5 37.3 %all-gather.3.cloned.1.call-start = ((), (), s32[]{:S(2)}) async-start(), calls=%async_computation.2 | async-start | bytes 1310720 | tf_op jit(solution)/shard_map/all_gather | solution.py:48
  6.5 0.7 copy-start.1
  7.4 0.8 copy-start
  9.0 10.2 %all-to-all-start = ((bf16[4,8,1024]{2,0,1:T(4,128)(2,1)}), bf16[4,8,1024]{2,0,1:T(4,128)(2,1)S(1)}, u32[]{:S(2)}, u32[]{:S(2)}) async-start(bf16[4,8,1024]{2,0,1:T(4,128)(2,1)} %copy.27), calls=%async_computation | async-start | bytes 131072 | tf_op jit(solution)/shard_map/all_to_all | solution.py:46
  43.9 0.7 copy-start.2
Sparse Core Ops, SparseCore 0:
  8.9 34.9 all-gather.2
where the time goes:
time: 177 us; the launch traced here: 174 us
  local copies, waits for them, and re-layouts  53.6 us (30%)
  other arithmetic  34.1 us (19%)
  matrix products  28.4 us (16%)
  blocking collectives  25.4 us (14%)
  between operations  13.5 us (8%)
  waiting for transfers between devices  12.7 us (7%)
  starting transfers between devices  5.2 us (3%)
    gather x16, local copies, waits for them, and re-layouts, one_tile(): near_f = jnp.take(all_f, index_row, axis=0)  29.9 us
    convert_element_type x16, other arithmetic, one_tile(): used = (slots < count).astype(jnp.float32)  21.5 us
    dot_general x16, matrix products, one_tile(): jnp.einsum('xq,kyq->kxy', own, near_f, preferred_element_type=jnp.float32)  17.1 us
    all_gather x1, blocking collectives, body(): lax.all_gather(local, 'ints', axis=1, tiled=True)  16.7 us
    select_n x16, other arithmetic, one_tile(): near_t = jnp.take(amp_tiles, index_row, axis=1)  11.1 us
    gather x16, local copies, waits for them, and re-layouts, one_tile(): near_t = jnp.take(amp_tiles, index_row, axis=1)  9.64 us
    dynamic_slice x16, local copies, waits for them, and re-layouts, tile_ladder(): stacked = lax.map(one_tile, (own_f, link_rows, count_rows))  9.38 us
    all_to_all x1, blocking collectives, body(): lax.all_to_all(rounded, 'pair', split_axis=0, concat_axis=1, tiled=True)  8.64 us
  transfers between devices with their start and end apart: 2, of which 2 were waited for; matrix products, arithmetic and copies ran while one was open for 1% of the time, Pallas kernels for 0%

commit v1 on v0

v1 whole, which is shorter than its diff:
```python
import functools

import jax
import jax.numpy as jnp
from jax import lax
from jax.experimental import pallas as pl
from jax.experimental.pallas import tpu as pltpu
from jax.sharding import PartitionSpec as P

ROWS = 8
DEPTH = 256


def iota(shape, dim):
    return lax.broadcasted_iota(jnp.int32, shape, dim)


def dot(a, b):
    return jnp.dot(a, b, preferred_element_type=jnp.float32)


def ones_where(cond):
    return jnp.where(cond, 1.0, 0.0).astype(jnp.bfloat16)


def kernel(
    np_, nz, t_hbm, m_hbm, f_hbm, l_hbm, c_hbm, o_ref,
    t_v, m_v, f_v, l_v, c_v, stage1, recv1, g_buf, li, stage2, recv2,
    in_sem, s1, r1, sg, rg, s2, r2,
):
    me = lax.axis_index("pair")
    mz = lax.axis_index("ints")
    pd, nb, width = t_v.shape
    tc, tile, nq = f_v.shape[1:]
    gt = nz * tc
    parts = ROWS // pd
    wh = width // parts
    nc = np_ * pd // ROWS
    gs = DEPTH // tile
    ng = tc // gs
    bf, f32 = jnp.bfloat16, jnp.float32

    loads = [
        pltpu.make_async_copy(src, dst, in_sem.at[i])
        for i, (src, dst) in enumerate(
            ((t_hbm, t_v), (m_hbm, m_v), (l_hbm, l_v), (c_hbm, c_v), (f_hbm, f_v))
        )
    ]
    for load in loads:
        load.start()

    barrier = pltpu.get_barrier_semaphore()
    for rel in range(1, np_):
        pl.semaphore_signal(
            barrier, inc=1, device_id={"pair": lax.rem(me + rel, np_)},
            device_id_type=pl.DeviceIdType.MESH,
        )
    has_left, has_right = mz > 0, mz < nz - 1

    @pl.when(has_left)
    def _():
        pl.semaphore_signal(
            barrier, inc=1, device_id={"ints": mz - 1}, device_id_type=pl.DeviceIdType.MESH
        )

    @pl.when(has_right)
    def _():
        pl.semaphore_signal(
            barrier, inc=1, device_id={"ints": mz + 1}, device_id_type=pl.DeviceIdType.MESH
        )

    loads[0].wait()
    loads[1].wait()
    spread = ones_where(
        (iota((tc, width), 1) >= iota((tc, width), 0) * tile)
        & (iota((tc, width), 1) < iota((tc, width), 0) * tile + tile)
    )
    amps = t_v[...].astype(f32).reshape(pd * nb, width)
    mask = m_v[...].astype(f32).reshape(pd * nb, tc).astype(bf)
    masked = (amps * dot(mask, spread)).astype(bf)
    piled = jnp.concatenate([masked[:, h * wh:(h + 1) * wh] for h in range(parts)], axis=0)
    shape = (nb * ROWS, ROWS * nb)
    row, col = iota(shape, 0), iota(shape, 1)
    order = ones_where(col == (row & (ROWS - 1)) * nb + lax.shift_right_logical(row, 3))
    slabs = dot(order, piled).reshape(nb, ROWS, wh).astype(bf)
    stage1[...] = slabs
    recv1[me] = stage1[me]

    to_wait = np_ - 1 + jnp.where(has_left, 1, 0) + jnp.where(has_right, 1, 0)
    pl.semaphore_wait(barrier, to_wait)

    def swap(stage, recv, ssem, rsem, peer, slot):
        return pltpu.make_async_remote_copy(
            src_ref=stage.at[peer], dst_ref=recv.at[slot],
            send_sem=ssem.at[peer], recv_sem=rsem.at[slot],
            device_id={"pair": peer}, device_id_type=pl.DeviceIdType.MESH,
        )

    for rel in range(1, np_):
        peer = lax.rem(me + rel, np_)
        swap(stage1, recv1, s1, r1, peer, me).start()

    loads[2].wait()
    loads[3].wait()
    links = l_v[0]
    eye = iota((tc, tc), 0) == iota((tc, tc), 1)
    counts = jnp.sum(
        jnp.where(eye, jnp.broadcast_to(c_v[...], (tc, tc)), 0), axis=1, keepdims=True
    )
    links = jnp.where(iota(links.shape, 1) < counts, links, -1)
    tiles = iota((tc, gt), 1)
    hits = jnp.zeros((tc, gt), f32)
    for k in range(links.shape[1]):
        hits = hits + jnp.where(links[:, k:k + 1] == tiles, 1.0, 0.0)
    rep = ones_where(
        lax.shift_right_logical(iota((tc * ROWS, tc), 0), 3) == iota((tc * ROWS, tc), 1)
    )
    tall = dot(rep, hits.astype(bf)).astype(bf)
    wide = (gt, gt * ROWS)
    across = ones_where(iota(wide, 0) == lax.shift_right_logical(iota(wide, 1), 3))
    full = (tc * ROWS, gt * ROWS)
    same = (iota(full, 0) & (ROWS - 1)) == (iota(full, 1) & (ROWS - 1))
    li[...] = jnp.where(same, dot(tall, across), 0.0).astype(bf)
    loads[4].wait()

    def hop(src, c, side):
        target = mz + 1 if side else mz - 1
        return pltpu.make_async_remote_copy(
            src_ref=g_buf.at[src, c], dst_ref=g_buf.at[src, c],
            send_sem=sg.at[side, src, c], recv_sem=rg.at[src, c],
            device_id={"ints": target}, device_id_type=pl.DeviceIdType.MESH,
        )

    lane_tile = lax.shift_right_logical(iota((ROWS, DEPTH), 1), tile.bit_length() - 1)
    sub = iota((ROWS, wh), 0)

    def chunk_of(i):
        return lax.rem(lax.div(me, parts) + i, nc)

    def shifted(x, by):
        by = by % ROWS
        return x if by == 0 else pltpu.roll(x, by, 0)

    def rows_of(pieces):
        out = pieces[0]
        for j in range(1, parts):
            out = jnp.where(sub >= j * pd, pieces[j], out)
        return out

    for i in range(nc):
        c = chunk_of(i)
        got = []
        for d in range(parts):
            dev = c * parts + d

            @pl.when(dev != me)
            def _(dev=dev):
                swap(stage1, recv1, s1, r1, dev, dev).wait_recv()

            got.append(dev)
        got = [recv1[dev].astype(f32) for dev in got]
        blocks = []
        for h in range(parts):
            part = rows_of([shifted(got[d], (d - h) * pd) for d in range(parts)])
            for j in range(wh // DEPTH):
                group = part[:, j * DEPTH:(j + 1) * DEPTH]
                lhs = jnp.concatenate(
                    [jnp.where(lane_tile == k, group, 0.0) for k in range(gs)], axis=0
                ).astype(bf)
                g = h * (wh // DEPTH) + j
                near = f_v[0, g * gs:(g + 1) * gs].reshape(DEPTH, nq)
                blocks.append(dot(lhs, near).astype(bf))
        g_buf[mz, c] = jnp.concatenate(blocks, axis=0)

        @pl.when(has_right)
        def _(c=c):
            hop(mz, c, 1).start()

        @pl.when(has_left)
        def _(c=c):
            hop(mz, c, 0).start()

    def take(dist, i, forward):
        c = chunk_of(i)

        @pl.when(mz - dist >= 0)
        def _():
            hop(mz - dist, c, 1).wait_recv()
            if forward:
                @pl.when(has_right)
                def _():
                    hop(mz - dist, c, 1).start()

        @pl.when(mz + dist < nz)
        def _():
            hop(mz + dist, c, 0).wait_recv()
            if forward:
                @pl.when(has_left)
                def _():
                    hop(mz + dist, c, 0).start()

    for dist in range(1, nz - 1):
        for i in range(nc):
            take(dist, i, True)

    for i in range(nc):
        c = chunk_of(i)
        if nz > 1:
            take(nz - 1, i, False)
        every = g_buf[:, c].reshape(gt * ROWS, nq)
        total = dot(li[...], every).astype(bf)
        flat = []
        for g in range(ng):
            near = f_v[0, g * gs:(g + 1) * gs].reshape(DEPTH, nq)
            mine = total[g * gs * ROWS:(g + 1) * gs * ROWS]
            crossed = lax.dot_general(
                mine, near, (((1,), (1,)), ((), ())), preferred_element_type=f32
            )
            kept = crossed[:ROWS]
            for k in range(1, gs):
                kept = jnp.where(lane_tile == k, crossed[k * ROWS:(k + 1) * ROWS], kept)
            flat.append(kept)
        flat = jnp.concatenate(flat, axis=1)
        halves = [flat[:, h * wh:(h + 1) * wh] for h in range(parts)]
        for d in range(parts):
            dev = c * parts + d
            slab = rows_of([shifted(halves[h], (h - d) * pd) for h in range(parts)])
            stage2[dev] = slab.astype(bf)

            @pl.when(dev != me)
            def _(dev=dev):
                swap(stage2, recv2, s2, r2, dev, me).start()

            @pl.when(dev == me)
            def _(dev=dev):
                recv2[dev] = stage2[dev]

    for rel in range(1, np_):
        peer = lax.rem(me + rel, np_)
        swap(stage2, recv2, s2, r2, peer, peer).wait_recv()
    landed = recv2[...].astype(f32).reshape(nb * ROWS, wh).astype(bf)
    shape = (pd * nb, nb * ROWS)
    row, col = iota(shape, 0), iota(shape, 1)
    for h in range(parts):
        back = ones_where(
            ((col & (ROWS - 1)) - h * pd) * nb + lax.shift_right_logical(col, 3) == row
        )
        o_ref[:, :, h * wh:(h + 1) * wh] = dot(back, landed).reshape(pd, nb, wh).astype(bf)

    for rel in range(1, np_):
        peer = lax.rem(me + rel, np_)
        swap(stage1, recv1, s1, r1, peer, me).wait_send()
        swap(stage2, recv2, s2, r2, peer, me).wait_send()
    for i in range(nc):
        for dist in range(nz - 1):
            @pl.when(has_right & (mz - dist >= 0))
            def _(i=i, dist=dist):
                hop(mz - dist, chunk_of(i), 1).wait_send()

            @pl.when(has_left & (mz + dist < nz))
            def _(i=i, dist=dist):
                hop(mz + dist, chunk_of(i), 0).wait_send()


def solution(mesh):
    np_, nz = mesh.shape["pair"], mesh.shape["ints"]

    def body(t_amps, block_mask, factors, links, link_counts):
        pd, nb, width = t_amps.shape
        _, tc, tile, nq = factors.shape
        parts = ROWS // pd
        nc = np_ * pd // ROWS
        slabs = (nb, ROWS, width // parts)
        bf = jnp.bfloat16
        return pl.pallas_call(
            functools.partial(kernel, np_, nz),
            out_shape=jax.ShapeDtypeStruct(t_amps.shape, bf),
            in_specs=[pl.BlockSpec(memory_space=pl.ANY)] * 5,
            out_specs=pl.BlockSpec(memory_space=pltpu.VMEM),
            scratch_shapes=[
                pltpu.VMEM(t_amps.shape, bf),
                pltpu.VMEM(block_mask.shape, jnp.int32),
                pltpu.VMEM(factors.shape, bf),
                pltpu.VMEM(links.shape, jnp.int32),
                pltpu.VMEM(link_counts.shape, jnp.int32),
                pltpu.VMEM(slabs, bf),
                pltpu.VMEM(slabs, bf),
                pltpu.VMEM((nz, nc, tc * ROWS, nq), bf),
                pltpu.VMEM((tc * ROWS, nz * tc * ROWS), bf),
                pltpu.VMEM(slabs, bf),
                pltpu.VMEM(slabs, bf),
                pltpu.SemaphoreType.DMA((5,)),
                pltpu.SemaphoreType.DMA((np_,)),
                pltpu.SemaphoreType.DMA((np_,)),
                pltpu.SemaphoreType.DMA((2, nz, nc)),
                pltpu.SemaphoreType.DMA((nz, nc)),
                pltpu.SemaphoreType.DMA((np_,)),
                pltpu.SemaphoreType.DMA((np_,)),
            ],
            compiler_params=pltpu.CompilerParams(collective_id=0, has_side_effects=True),
        )(t_amps, block_mask, factors, links, link_counts)

    placed = (
        P("pair", None, "ints"),
        P("pair", None, "ints"),
        P("pair", "ints", None, None),
        P("pair", "ints", None),
        P("pair", "ints"),
    )
    return jax.shard_map(
        body, mesh=mesh, in_specs=placed, out_specs=P("pair", None, "ints"), check_vma=False
    )
```

time: 177 us -> 24.8 us (0.14); the launches traced: 174 us -> 24.6 us
  local copies, waits for them, and re-layouts: 53.6 us -> 1.47 us
  other arithmetic: 34.1 us -> 0 us
  matrix products: 28.4 us -> 0 us
  blocking collectives: 25.4 us -> 0 us
  Pallas kernels: 0 us -> 23.1 us
  between operations: 13.5 us -> 0.01 us
  waiting for transfers between devices: 12.7 us -> 0 us
  starting transfers between devices: 5.2 us -> 0 us
    gather x32 -> x0, local copies, waits for them, and re-layouts: 39.6 us -> none  [the longest x16 29.9 us: one_tile(): near_f = jnp.take(all_f, index_row, axis=0)]
    dot_general x48 -> x0, matrix products: 28.4 us -> none  [the longest x16 17.1 us: one_tile(): jnp.einsum('xq,kyq->kxy', own, near_f, preferred_element_type=jnp.float32)]
    pallas_call x0 -> x1, Pallas kernels: none -> 23.1 us  [body(): pl.pallas_call(functools.partial(kernel, np_, nz), out_shape=jax.ShapeDty...]
    convert_element_type x18 -> x0, other arithmetic: 22.5 us -> none  [the longest x16 21.5 us: one_tile(): used = (slots < count).astype(jnp.float32)]
    all_gather x1 -> x0, blocking collectives: 16.7 us -> none  [body(): lax.all_gather(local, 'ints', axis=1, tiled=True)]
    select_n x16 -> x0, other arithmetic: 11.1 us -> none  [one_tile(): near_t = jnp.take(amp_tiles, index_row, axis=1)]
    dynamic_slice x16 -> x0, local copies, waits for them, and re-layouts: 9.38 us -> none  [tile_ladder(): stacked = lax.map(one_tile, (own_f, link_rows, count_rows))]
    all_to_all x1 -> x0, blocking collectives: 8.64 us -> none  [body(): lax.all_to_all(rounded, 'pair', split_axis=0, concat_axis=1, tiled=True)]
  transfers between devices with their start and end apart: 2 -> 0, of which waited for: 2 -> 0; matrix products, arithmetic and copies ran while one was open for 1% -> 0% of each run, Pallas kernels for 0% -> 0%
where the time goes in v1:
time: 24.8 us; the launch traced here: 24.6 us
  Pallas kernels  23.1 us (93%)
  local copies, waits for them, and re-layouts  1.47 us (6%)
    pallas_call x1, Pallas kernels, body(): pl.pallas_call(functools.partial(kernel, np_, nz), out_shape=jax.ShapeDty...  23.1 us
    unnamed x1, local copies, waits for them, and re-layouts  1.47 us

profile of v1, /device:TPU:0, one launch (start us, length us, event | category | flops | bytes accessed | tf_op | source)
XLA Modules:
  0.0 24.6 jit_solution(8881522855597877932)
XLA Ops:
  0.0 23.1 %shard_map.55 = bf16[4,8,1024]{2,1,0:T(8,128)(2,1)} custom-call(bf16[4,8,1024]{2,1,0:T(8,128)(2,1)} %t_hbm.1, s32[4,8,16]{2,1,0:T(8,128)} %m_hbm.1, bf16[1,16,64,128]{3,2,1,0:T(8,128)(2,1)} %f_hbm.1, s32[1,16,32]{2,1,0:T(8,128)} %l_hbm.1, s32[1,16]{1,0:T(1,128)} %c_hbm.1), custom_call_target="tpu_custom_call" | custom-call | tf_op jit(solution)/shard_map/pallas_call | solution.py:275
  23.1 1.5 %copy.7 = bf16[4,8,1024]{2,1,0:T(8,128)(2,1)} copy(bf16[4,8,1024]{2,1,0:T(8,128)(2,1)} %shard_map.55) | data formatting | bytes 131072

commit v2 on v1

--- a/solution.py
+++ b/solution.py
@@ -26,7 +26,7 @@
 def kernel(
     np_, nz, t_hbm, m_hbm, f_hbm, l_hbm, c_hbm, o_ref,
     t_v, m_v, f_v, l_v, c_v, stage1, recv1, g_buf, li, stage2, recv2,
-    in_sem, s1, r1, sg, rg, s2, r2,
+    l_end, c_end, li_end, p_out, p_in, tot, in_sem, s1, r1, sg, rg, s2, r2, se, re, sp, rp,
 ):
     me = lax.axis_index("pair")
     mz = lax.axis_index("ints")
@@ -55,18 +55,10 @@
             barrier, inc=1, device_id={"pair": lax.rem(me + rel, np_)},
             device_id_type=pl.DeviceIdType.MESH,
         )
-    has_left, has_right = mz > 0, mz < nz - 1
-
-    @pl.when(has_left)
-    def _():
+    for rel in range(1, nz):
         pl.semaphore_signal(
-            barrier, inc=1, device_id={"ints": mz - 1}, device_id_type=pl.DeviceIdType.MESH
-        )
-
-    @pl.when(has_right)
-    def _():
-        pl.semaphore_signal(
-            barrier, inc=1, device_id={"ints": mz + 1}, device_id_type=pl.DeviceIdType.MESH
+            barrier, inc=1, device_id={"ints": lax.rem(mz + rel, nz)},
+            device_id_type=pl.DeviceIdType.MESH,
         )
 
     loads[0].wait()
@@ -86,8 +78,7 @@
     stage1[...] = slabs
     recv1[me] = stage1[me]
 
-    to_wait = np_ - 1 + jnp.where(has_left, 1, 0) + jnp.where(has_right, 1, 0)
-    pl.semaphore_wait(barrier, to_wait)
+    pl.semaphore_wait(barrier, np_ + nz - 2)
 
     def swap(stage, recv, ssem, rsem, peer, slot):
         return pltpu.make_async_remote_copy(
@@ -102,33 +93,71 @@
 
     loads[2].wait()
     loads[3].wait()
-    links = l_v[0]
-    eye = iota((tc, tc), 0) == iota((tc, tc), 1)
-    counts = jnp.sum(
-        jnp.where(eye, jnp.broadcast_to(c_v[...], (tc, tc)), 0), axis=1, keepdims=True
-    )
-    links = jnp.where(iota(links.shape, 1) < counts, links, -1)
-    tiles = iota((tc, gt), 1)
-    hits = jnp.zeros((tc, gt), f32)
-    for k in range(links.shape[1]):
-        hits = hits + jnp.where(links[:, k:k + 1] == tiles, 1.0, 0.0)
-    rep = ones_where(
-        lax.shift_right_logical(iota((tc * ROWS, tc), 0), 3) == iota((tc * ROWS, tc), 1)
-    )
-    tall = dot(rep, hits.astype(bf)).astype(bf)
-    wide = (gt, gt * ROWS)
-    across = ones_where(iota(wide, 0) == lax.shift_right_logical(iota(wide, 1), 3))
-    full = (tc * ROWS, gt * ROWS)
-    same = (iota(full, 0) & (ROWS - 1)) == (iota(full, 1) & (ROWS - 1))
-    li[...] = jnp.where(same, dot(tall, across), 0.0).astype(bf)
+    is_end = [mz == 0, mz == nz - 1]
+    helps = [mz == 1, mz == nz - 2]
+
+    def tell(side, j):
+        src, dst = ((l_v, l_end.at[side]), (c_v, c_end.at[side]))[j]
+        return pltpu.make_async_remote_copy(
+            src_ref=src, dst_ref=dst, send_sem=se.at[side, j], recv_sem=re.at[side, j],
+            device_id={"ints": mz - 1 if side else mz + 1},
+            device_id_type=pl.DeviceIdType.MESH,
+        )
+
+    for side in range(2):
+        @pl.when(is_end[side])
+        def _(side=side):
+            tell(side, 0).start()
+            tell(side, 1).start()
+
+    def spread_links(links, counts):
+        eye = iota((tc, tc), 0) == iota((tc, tc), 1)
+        counts = jnp.sum(
+            jnp.where(eye, jnp.broadcast_to(counts, (tc, tc)), 0), axis=1, keepdims=True
+        )
+        links = jnp.where(iota(links.shape, 1) < counts, links, -1)
+        tiles = iota((tc, gt), 1)
+        hits = jnp.zeros((tc, gt), f32)
+        for k in range(links.shape[1]):
+            hits = hits + jnp.where(links[:, k:k + 1] == tiles, 1.0, 0.0)
+        rep = ones_where(
+            lax.shift_right_logical(iota((tc * ROWS, tc), 0), 3) == iota((tc * ROWS, tc), 1)
+        )
+        tall = dot(rep, hits.astype(bf)).astype(bf)
+        wide = (gt, gt * ROWS)
+        across = ones_where(iota(wide, 0) == lax.shift_right_logical(iota(wide, 1), 3))
+        full = (tc * ROWS, gt * ROWS)
+        same = (iota(full, 0) & (ROWS - 1)) == (iota(full, 1) & (ROWS - 1))
+        return jnp.where(same, dot(tall, across), 0.0).astype(bf)
+
+    li[...] = spread_links(l_v[0], c_v[...])
+    for side in range(2):
+        @pl.when(helps[side])
+        def _(side=side):
+            tell(side, 0).wait_recv()
+            tell(side, 1).wait_recv()
+            li_end[side] = spread_links(l_end[side, 0], c_end[side])
+
     loads[4].wait()
 
-    def hop(src, c, side):
-        target = mz + 1 if side else mz - 1
+    def inner(z):
+        return (z > 0) & (z < nz - 1)
+
+    def spread_to(target, src, c):
         return pltpu.make_async_remote_copy(
-            src_ref=g_buf.at[src, c], dst_ref=g_buf.at[src, c],
-            send_sem=sg.at[side, src, c], recv_sem=rg.at[src, c],
+            src_ref=g_buf.at[mz, c], dst_ref=g_buf.at[src, c],
+            send_sem=sg.at[target, c], recv_sem=rg.at[src, c],
             device_id={"ints": target}, device_id_type=pl.DeviceIdType.MESH,
+        )
+
+    others = [lax.rem(mz + rel, nz) for rel in range(1, nz)]
+
+    def sum_hop(c, side):
+        return pltpu.make_async_remote_copy(
+            src_ref=p_out.at[side, c], dst_ref=p_in.at[c],
+            send_sem=sp.at[side, c], recv_sem=rp.at[c],
+            device_id={"ints": mz + 1 if side else mz - 1},
+            device_id_type=pl.DeviceIdType.MESH,
         )
 
     lane_tile = lax.shift_right_logical(iota((ROWS, DEPTH), 1), tile.bit_length() - 1)
@@ -172,43 +201,42 @@
                 blocks.append(dot(lhs, near).astype(bf))
         g_buf[mz, c] = jnp.concatenate(blocks, axis=0)
 
-        @pl.when(has_right)
-        def _(c=c):
-            hop(mz, c, 1).start()
-
-        @pl.when(has_left)
-        def _(c=c):
-            hop(mz, c, 0).start()
-
-    def take(dist, i, forward):
-        c = chunk_of(i)
-
-        @pl.when(mz - dist >= 0)
-        def _():
-            hop(mz - dist, c, 1).wait_recv()
-            if forward:
-                @pl.when(has_right)
-                def _():
-                    hop(mz - dist, c, 1).start()
-
-        @pl.when(mz + dist < nz)
-        def _():
-            hop(mz + dist, c, 0).wait_recv()
-            if forward:
-                @pl.when(has_left)
-                def _():
-                    hop(mz + dist, c, 0).start()
-
-    for dist in range(1, nz - 1):
-        for i in range(nc):
-            take(dist, i, True)
-
+        for target in others:
+            @pl.when(inner(target))
+            def _(target=target, c=c):
+                spread_to(target, mz, c).start()
+
+    part_rows = tc * ROWS
     for i in range(nc):
         c = chunk_of(i)
-        if nz > 1:
-            take(nz - 1, i, False)
-        every = g_buf[:, c].reshape(gt * ROWS, nq)
-        total = dot(li[...], every).astype(bf)
+
+        @pl.when(inner(mz))
+        def _(c=c):
+            for src in others:
+                spread_to(src, src, c).wait_recv()
+
+        for side in range(2):
+            @pl.when(helps[side])
+            def _(c=c, side=side):
+                first, last = (0, nz - 1) if side else (1, nz)
+                near = g_buf[first:last, c].reshape((last - first) * part_rows, nq)
+                cols = li_end[side, :, first * part_rows:last * part_rows]
+                p_out[side, c] = dot(cols, near).astype(bf)
+                sum_hop(c, side).start()
+
+        for side in range(2):
+            @pl.when(is_end[side])
+            def _(c=c, side=side):
+                own = (nz - 1) * side
+                mine = dot(li[:, own * part_rows:(own + 1) * part_rows], g_buf[own, c])
+                sum_hop(c, side).wait_recv()
+                tot[...] = mine + p_in[c].astype(f32)
+
+        @pl.when(inner(mz))
+        def _(c=c):
+            tot[...] = dot(li[...], g_buf[:, c].reshape(gt * ROWS, nq))
+
+        total = tot[...].astype(bf)
         flat = []
         for g in range(ng):
             near = f_v[0, g * gs:(g + 1) * gs].reshape(DEPTH, nq)
@@ -251,15 +279,22 @@
         peer = lax.rem(me + rel, np_)
         swap(stage1, recv1, s1, r1, peer, me).wait_send()
         swap(stage2, recv2, s2, r2, peer, me).wait_send()
+    for side in range(2):
+        @pl.when(is_end[side])
+        def _(side=side):
+            tell(side, 0).wait_send()
+            tell(side, 1).wait_send()
+
     for i in range(nc):
-        for dist in range(nz - 1):
-            @pl.when(has_right & (mz - dist >= 0))
-            def _(i=i, dist=dist):
-                hop(mz - dist, chunk_of(i), 1).wait_send()
-
-            @pl.when(has_left & (mz + dist < nz))
-            def _(i=i, dist=dist):
-                hop(mz + dist, chunk_of(i), 0).wait_send()
+        for target in others:
+            @pl.when(inner(target))
+            def _(target=target, i=i):
+                spread_to(target, mz, chunk_of(i)).wait_send()
+
+        for side in range(2):
+            @pl.when(helps[side])
+            def _(i=i, side=side):
+                sum_hop(chunk_of(i), side).wait_send()
 
 
 def solution(mesh):
@@ -274,7 +309,7 @@
         bf = jnp.bfloat16
         return pl.pallas_call(
             functools.partial(kernel, np_, nz),
-            out_shape=jax.ShapeDtypeStruct(t_amps.shape, bf),
+            out_shape=pltpu.VMEM(t_amps.shape, bf),
             in_specs=[pl.BlockSpec(memory_space=pl.ANY)] * 5,
             out_specs=pl.BlockSpec(memory_space=pltpu.VMEM),
             scratch_shapes=[
@@ -289,13 +324,23 @@
                 pltpu.VMEM((tc * ROWS, nz * tc * ROWS), bf),
                 pltpu.VMEM(slabs, bf),
                 pltpu.VMEM(slabs, bf),
+                pltpu.VMEM((2,) + links.shape, jnp.int32),
+                pltpu.VMEM((2,) + link_counts.shape, jnp.int32),
+                pltpu.VMEM((2, tc * ROWS, nz * tc * ROWS), bf),
+                pltpu.VMEM((2, nc, tc * ROWS, nq), bf),
+                pltpu.VMEM((nc, tc * ROWS, nq), bf),
+                pltpu.VMEM((tc * ROWS, nq), jnp.float32),
                 pltpu.SemaphoreType.DMA((5,)),
                 pltpu.SemaphoreType.DMA((np_,)),
                 pltpu.SemaphoreType.DMA((np_,)),
-                pltpu.SemaphoreType.DMA((2, nz, nc)),
+                pltpu.SemaphoreType.DMA((nz, nc)),
                 pltpu.SemaphoreType.DMA((nz, nc)),
                 pltpu.SemaphoreType.DMA((np_,)),
                 pltpu.SemaphoreType.DMA((np_,)),
+                pltpu.SemaphoreType.DMA((2, 2)),
+                pltpu.SemaphoreType.DMA((2, 2)),
+                pltpu.SemaphoreType.DMA((2, nc)),
+                pltpu.SemaphoreType.DMA((nc,)),
             ],
             compiler_params=pltpu.CompilerParams(collective_id=0, has_side_effects=True),
         )(t_amps, block_mask, factors, links, link_counts)

time: 24.8 us -> 22.7 us (0.915)
  Pallas kernels: 23.1 us -> 21.9 us
  local copies, waits for them, and re-layouts: 1.47 us -> 0.63 us
    pallas_call x1, Pallas kernels: 23.1 us -> 21.9 us  [body(): pl.pallas_call(functools.partial(kernel, np_, nz), out_shape=pltpu.VMEM(t...]
    unnamed x1, local copies, waits for them, and re-layouts: 1.47 us -> 0.63 us
where the time goes in v2:
time: 22.7 us; the launch traced here: 22.6 us
  Pallas kernels  21.9 us (96%)
  local copies, waits for them, and re-layouts  0.63 us (3%)
    pallas_call x1, Pallas kernels, body(): pl.pallas_call(functools.partial(kernel, np_, nz), out_shape=pltpu.VMEM(t...  21.9 us
    unnamed x1, local copies, waits for them, and re-layouts  0.63 us

profile of v2, /device:TPU:0, one launch (start us, length us, event | category | flops | bytes accessed | tf_op | source)
XLA Modules:
  0.0 22.6 jit_solution(4049452756968078905)
XLA Ops:
  0.0 21.9 %shard_map.55 = bf16[4,8,1024]{2,1,0:T(8,128)(2,1)S(1)} custom-call(bf16[4,8,1024]{2,1,0:T(8,128)(2,1)} %t_hbm.1, s32[4,8,16]{2,1,0:T(8,128)} %m_hbm.1, bf16[1,16,64,128]{3,2,1,0:T(8,128)(2,1)} %f_hbm.1, s32[1,16,32]{2,1,0:T(8,128)} %l_hbm.1, s32[1,16]{1,0:T(1,128)} %c_hbm.1), custom_call_target="tpu_custom_call" | custom-call | tf_op jit(solution)/shard_map/pallas_call | solution.py:310
  22.0 0.6 %copy.7 = bf16[4,8,1024]{2,1,0:T(8,128)(2,1)} copy(bf16[4,8,1024]{2,1,0:T(8,128)(2,1)S(1)} %shard_map.55) | data formatting | bytes 131072

commit v3 on v2

--- a/solution.py
+++ b/solution.py
@@ -55,11 +55,24 @@
             barrier, inc=1, device_id={"pair": lax.rem(me + rel, np_)},
             device_id_type=pl.DeviceIdType.MESH,
         )
-    for rel in range(1, nz):
-        pl.semaphore_signal(
-            barrier, inc=1, device_id={"ints": lax.rem(mz + rel, nz)},
-            device_id_type=pl.DeviceIdType.MESH,
-        )
+
+    def inner(z):
+        return (z > 0) & (z < nz - 1)
+
+    def close(a, b):
+        return inner(b) | (b == 0) & (a == 1) | (b == nz - 1) & (a == nz - 2)
+
+    others = [lax.rem(mz + rel, nz) for rel in range(1, nz)]
+    to_wait = np_ - 1
+    for other in others:
+        to_wait = to_wait + jnp.where(close(mz, other), 1, 0)
+
+        @pl.when(close(other, mz))
+        def _(other=other):
+            pl.semaphore_signal(
+                barrier, inc=1, device_id={"ints": other},
+                device_id_type=pl.DeviceIdType.MESH,
+            )
 
     loads[0].wait()
     loads[1].wait()
@@ -78,7 +91,7 @@
     stage1[...] = slabs
     recv1[me] = stage1[me]
 
-    pl.semaphore_wait(barrier, np_ + nz - 2)
+    pl.semaphore_wait(barrier, to_wait)
 
     def swap(stage, recv, ssem, rsem, peer, slot):
         return pltpu.make_async_remote_copy(
@@ -130,18 +143,7 @@
         same = (iota(full, 0) & (ROWS - 1)) == (iota(full, 1) & (ROWS - 1))
         return jnp.where(same, dot(tall, across), 0.0).astype(bf)
 
-    li[...] = spread_links(l_v[0], c_v[...])
-    for side in range(2):
-        @pl.when(helps[side])
-        def _(side=side):
-            tell(side, 0).wait_recv()
-            tell(side, 1).wait_recv()
-            li_end[side] = spread_links(l_end[side, 0], c_end[side])
-
     loads[4].wait()
-
-    def inner(z):
-        return (z > 0) & (z < nz - 1)
 
     def spread_to(target, src, c):
         return pltpu.make_async_remote_copy(
@@ -149,8 +151,6 @@
             send_sem=sg.at[target, c], recv_sem=rg.at[src, c],
             device_id={"ints": target}, device_id_type=pl.DeviceIdType.MESH,
         )
-
-    others = [lax.rem(mz + rel, nz) for rel in range(1, nz)]
 
     def sum_hop(c, side):
         return pltpu.make_async_remote_copy(
@@ -206,6 +206,14 @@
             def _(target=target, c=c):
                 spread_to(target, mz, c).start()
 
+    for side in range(2):
+        @pl.when(helps[side])
+        def _(side=side):
+            tell(side, 0).wait_recv()
+            tell(side, 1).wait_recv()
+            li_end[side] = spread_links(l_end[side, 0], c_end[side])
+
+    li[...] = spread_links(l_v[0], c_v[...])
     part_rows = tc * ROWS
     for i in range(nc):
         c = chunk_of(i)

time: 22.7 us -> 22.7 us (level)
  no operation moved by 1% of the time
where the time goes in v3:
time: 22.7 us; the launch traced here: 22.6 us
  Pallas kernels  22 us (97%)
  local copies, waits for them, and re-layouts  0.63 us (3%)
    pallas_call x1, Pallas kernels, body(): pl.pallas_call(functools.partial(kernel, np_, nz), out_shape=pltpu.VMEM(t...  22 us
    unnamed x1, local copies, waits for them, and re-layouts  0.63 us

profile of v3, /device:TPU:0, one launch (start us, length us, event | category | flops | bytes accessed | tf_op | source)
XLA Modules:
  0.0 22.6 jit_solution(5555294217990963722)
XLA Ops:
  0.0 22.0 %shard_map.55 = bf16[4,8,1024]{2,1,0:T(8,128)(2,1)S(1)} custom-call(bf16[4,8,1024]{2,1,0:T(8,128)(2,1)} %t_hbm.1, s32[4,8,16]{2,1,0:T(8,128)} %m_hbm.1, bf16[1,16,64,128]{3,2,1,0:T(8,128)(2,1)} %f_hbm.1, s32[1,16,32]{2,1,0:T(8,128)} %l_hbm.1, s32[1,16]{1,0:T(1,128)} %c_hbm.1), custom_call_target="tpu_custom_call" | custom-call | tf_op jit(solution)/shard_map/pallas_call | solution.py:318
  22.0 0.6 %copy.7 = bf16[4,8,1024]{2,1,0:T(8,128)(2,1)} copy(bf16[4,8,1024]{2,1,0:T(8,128)(2,1)S(1)} %shard_map.55) | data formatting | bytes 131072
